TPU v7x, 128 devices: a whole 4x4x4 slice. The times are simulated.
128 devices in a mesh: req: 16 (over z, x), head: 8 (over y, core).
Axes of the slice: x: 4, y: 4, z: 4, core: 2. Of those that a mesh axis runs over, the one named last changes fastest.
Arguments:
- hidden_in: bfloat16 [16384, 2048], P(('req', 'head')), may hold values from -1.5 to 1.5
- attn_gain: float32 [2048], replicated, may hold values from 0.1 to 1.9
- query_weight: bfloat16 [2048, 3072], P(None, 'head'), may hold values from -0.25 to 0.25
- latent_weight: bfloat16 [2048, 512], replicated, may hold values from -0.125 to 0.125
- rope_key_weight: bfloat16 [64, 2048], replicated, may hold values from -0.125 to 0.125
- latent_gain: float32 [512], replicated, may hold values from 0.1 to 1.9
- kv_up_weight: bfloat16 [512, 4096], P(None, 'head'), may hold values from -0.25 to 0.25
- out_weight: bfloat16 [2048, 2048], P('head'), may hold values from -0.5 to 0.5
- pool_latent: bfloat16 [256, 128, 512], P('req'), may hold values from -1.6953125 to 1.6953125
- pool_rope: bfloat16 [256, 64, 128], P('req'), may hold values from -1.6953125 to 1.6953125
- page_table: int32 [16, 16], P('req'), may hold values from 0 to 15, each once within a row
- cache_len: int32 [16], P('req'), may hold values from 1 to 2048, 16384 in all
- post_gain: float32 [2048], replicated, may hold values from 0.1 to 1.9
- router_weight: bfloat16 [2048, 64], replicated, may hold values from -0.125 to 0.125
- routes: int32 [16384, 6], P(('req', 'head')), may hold values from 0 to 63, all different within a row; in each aligned block of 128 rows (0 to 127, 128 to 255, ...) at most 14 rows name the same one
- shared_gate_up: bfloat16 [2, 2048, 2816], P(None, None, 'head'), may hold values from -0.125 to 0.125
- shared_down: bfloat16 [2816, 2048], P('head'), may hold values from -0.109375 to 0.109375
- expert_gate_up: bfloat16 [128, 2, 2048, 704], P(('req', 'head')), may hold values from -0.125 to 0.125
- expert_down: bfloat16 [128, 704, 2048], P(('req', 'head')), may hold values from -1.25 to 1.25
Outputs:
- hidden_out: bfloat16 [16384, 2048], P(('req', 'head'))
- latent_new: bfloat16 [16384, 512], P(('req', 'head'))
- rope_new: bfloat16 [64, 16384], P(None, ('req', 'head'))
Inputs may be any that keep to these rules, and one draw needn't show every extreme that they name: `routes`: in each aligned block of 128 rows (the rows of one device), no expert is named by more than 14 rows, a bound that some block reaches; the 6 entries of a row differ. Each row is a permutation; entry p of row r is the page, row r * 16 + page_table[r, p] of the pools, that holds cached positions p * 128 to (p + 1) * 128 - 1 of request r. `cache_len`: the lengths sum to 16384, and one of them is 2048.
All inputs are finite; a program needn't handle non-finite values. No bound on the sum of `cache_len` on one device may be relied on, other than what follows from the above.
Results may differ from a plain program's by a relative error of at most 0.03.
Values may be sent and summed in bfloat16 or wider, within the bound.
A program may use at most 128 MiB of HBM per device.

v0:
```python
import math

import jax
import jax.numpy as jnp
from jax import lax
from jax.sharding import Mesh, PartitionSpec as P


HEAD_NOPE = 128
ROPE = 64
VDIM = 128
LATENT = 512
EXPERTS = 64
TOP = 6
HEAD_AXES = ("y", "core")
CHIP_AXES = ("req", "y")


EPSILON = 1e-06
THETA = 10000.0


def rms_norm(values, weights):
    widened = values.astype(jnp.float32)
    factor = lax.rsqrt(jnp.mean(widened * widened, axis=-1, keepdims=True) + EPSILON)
    return widened * factor * weights


def frequency_table(entries):
    return THETA ** (-2.0 * jnp.arange(entries // 2, dtype=jnp.float32) / entries)


def rotary_rows(values, places):
    halfway = values.shape[-1] // 2
    angles = places[:, None, None] * frequency_table(values.shape[-1])[None, None, :]
    cosine = jnp.cos(angles)
    sine_of = jnp.sin(angles)
    first_half = values[..., :halfway]
    second_half = values[..., halfway:]
    return jnp.concatenate(
        [first_half * cosine - second_half * sine_of, first_half * sine_of + second_half * cosine],
        axis=-1,
    )


def rotary_columns(values, places):
    halfway = values.shape[0] // 2
    angles = places[None, :] * frequency_table(values.shape[0])[:, None]
    cosine = jnp.cos(angles)
    sine_of = jnp.sin(angles)
    first_half = values[:halfway]
    second_half = values[halfway:]
    return jnp.concatenate(
        [first_half * cosine - second_half * sine_of, first_half * sine_of + second_half * cosine],
        axis=0,
    )


def body(
    hidden_in,
    attn_gain,
    query_weight,
    latent_weight,
    rope_key_weight,
    latent_gain,
    kv_up_weight,
    out_weight,
    pool_latent,
    pool_rope,
    page_table,
    cache_len,
    post_gain,
    router_weight,
    routes,
    shared_gate_up,
    shared_down,
    expert_gate_up,
    expert_down,
):
    swap = [(0, 1), (1, 0)]
    mate_gate_up = lax.ppermute(expert_gate_up, "core", swap)
    mate_down = lax.ppermute(expert_down, "core", swap)
    groups = lax.axis_size("y") * lax.axis_size("core")
    member = lax.axis_index("y") * lax.axis_size("core") + lax.axis_index("core")
    own_rows = hidden_in.shape[0]
    fresh_count = own_rows * groups
    model_width = hidden_in.shape[1]
    head_width = HEAD_NOPE + ROPE
    local_heads = query_weight.shape[1] // head_width
    length = cache_len[0]
    own_start = member * own_rows
    offsets = jnp.arange(fresh_count, dtype=jnp.int32)
    places = (length + offsets).astype(jnp.float32)
    own_places = lax.dynamic_slice_in_dim(places, own_start, own_rows, 0)
    gathered = lax.all_gather(hidden_in, HEAD_AXES, axis=0, tiled=True)
    normed = rms_norm(gathered, attn_gain).astype(jnp.bfloat16)
    own_normed = lax.dynamic_slice_in_dim(normed, own_start, own_rows, 0)
    latent_raw = jnp.dot(own_normed, latent_weight, preferred_element_type=jnp.float32)
    latent_rows = rms_norm(latent_raw, latent_gain).astype(jnp.bfloat16)
    rope_raw = jnp.einsum(
        "rd,nd->rn", rope_key_weight, own_normed, preferred_element_type=jnp.float32
    )
    own_rope = rotary_columns(rope_raw, own_places).astype(jnp.bfloat16)
    fresh_latent, fresh_rope = (
        lax.all_gather(latent_rows, HEAD_AXES, axis=0, tiled=True),
        lax.all_gather(own_rope, HEAD_AXES, axis=1, tiled=True),
    )
    queries = jnp.dot(normed, query_weight, preferred_element_type=jnp.float32).reshape(
        fresh_count, local_heads, head_width
    )
    query_nope = queries[..., :HEAD_NOPE].astype(jnp.bfloat16)
    query_rope = rotary_rows(queries[..., HEAD_NOPE:], places).astype(jnp.bfloat16)
    scale_factor = float(head_width) ** (-0.5)

    def score_block(keys_latent, keys_rope):
        keys_up = jnp.dot(keys_latent, kv_up_weight, preferred_element_type=jnp.float32).astype(
            jnp.bfloat16
        )
        keys_up = keys_up.reshape(keys_latent.shape[0], local_heads, HEAD_NOPE + VDIM)
        scores = jnp.einsum(
            "thc,khc->htk", query_nope, keys_up[..., :HEAD_NOPE], preferred_element_type=jnp.float32
        )
        scores = (
            scores
            + jnp.einsum("thc,ck->htk", query_rope, keys_rope, preferred_element_type=jnp.float32)
        ) * scale_factor
        return (scores, keys_up[..., HEAD_NOPE:])

    def accumulate(running, scores, allowed, values):
        totals, mixture = running
        weights = jnp.where(allowed, jnp.exp(scores), 0.0)
        mixture = mixture + jnp.einsum(
            "htk,khv->thv", weights.astype(jnp.bfloat16), values, preferred_element_type=jnp.float32
        )
        return (totals + jnp.sum(weights, axis=-1), mixture)

    table_row = page_table[0]
    cache_rows = pool_latent.shape[0] * pool_latent.shape[1]
    cached_latent = pool_latent[table_row].reshape(cache_rows, LATENT)
    cached_rope = jnp.transpose(pool_rope[table_row], (1, 0, 2)).reshape(ROPE, cache_rows)
    stride = math.gcd(cache_rows, 512)

    def cache_step(position, running):
        first_row = position * stride
        keys_latent = lax.dynamic_slice_in_dim(cached_latent, first_row, stride, 0)
        keys_rope = lax.dynamic_slice_in_dim(cached_rope, first_row, stride, 1)
        scores, values = score_block(keys_latent, keys_rope)
        allowed = (first_row + jnp.arange(stride, dtype=jnp.int32) < length)[None, None, :]
        return accumulate(running, scores, allowed, values)

    start_state = (
        jnp.zeros((local_heads, fresh_count), jnp.float32),
        jnp.zeros((fresh_count, local_heads, VDIM), jnp.float32),
    )
    used_blocks = (length + stride - 1) // stride
    running = lax.fori_loop(0, used_blocks, cache_step, start_state)
    scores, values = score_block(fresh_latent, fresh_rope)
    allowed = (offsets[None, :] <= offsets[:, None])[None]
    totals, mixture = accumulate(running, scores, allowed, values)
    attended = (
        (mixture / jnp.transpose(totals)[..., None])
        .astype(jnp.bfloat16)
        .reshape(fresh_count, local_heads * VDIM)
    )
    rows_block = attended
    attn_sum = lax.psum_scatter(
        jnp.dot(rows_block, out_weight, preferred_element_type=jnp.float32).astype(jnp.bfloat16),
        HEAD_AXES,
        scatter_dimension=0,
        tiled=True,
    ).astype(jnp.float32)
    residual = (hidden_in.astype(jnp.float32) + attn_sum).astype(jnp.bfloat16)
    post_own = rms_norm(residual, post_gain).astype(jnp.bfloat16)
    piece = lax.all_gather(post_own, HEAD_AXES, axis=0, tiled=True)
    gate_part = jnp.dot(piece, shared_gate_up[0], preferred_element_type=jnp.float32)
    up_part = jnp.dot(piece, shared_gate_up[1], preferred_element_type=jnp.float32)
    inner_rows = (jax.nn.silu(gate_part) * up_part).astype(jnp.bfloat16)
    rows_block = inner_rows
    shared = lax.psum_scatter(
        jnp.dot(rows_block, shared_down, preferred_element_type=jnp.float32).astype(jnp.bfloat16),
        HEAD_AXES,
        scatter_dimension=0,
        tiled=True,
    ).astype(jnp.float32)
    logits = jnp.dot(post_own, router_weight, preferred_element_type=jnp.float32)
    picker = routes[:, :, None] == jnp.arange(EXPERTS, dtype=jnp.int32)[None, None, :]
    chosen_logits = jnp.sum(jnp.where(picker, logits[:, None, :], 0.0), axis=-1)
    raised = jnp.exp(chosen_logits)
    gate_share = raised / jnp.sum(raised, axis=1, keepdims=True)
    capacity = -(-max(2, own_rows * 7 // 64) // 16) * 16
    slots = EXPERTS * capacity
    flat_routes = routes.reshape(own_rows * TOP)
    onehot = (flat_routes[:, None] == jnp.arange(EXPERTS, dtype=jnp.int32)[None, :]).astype(
        jnp.int32
    )
    slot_rank = jnp.sum((jnp.cumsum(onehot, axis=0, dtype=jnp.int32) - onehot) * onehot, axis=1)
    slot_id = (flat_routes * capacity + slot_rank).reshape(own_rows, TOP)
    picked = slot_id[:, :, None] == jnp.arange(slots, dtype=jnp.int32)[None, None, :]
    dispatch = jnp.any(picked, axis=1).astype(jnp.bfloat16)
    combine = jnp.sum(jnp.where(picked, gate_share[:, :, None], 0.0), axis=1)
    combine_hi = combine.astype(jnp.bfloat16)
    combine_lo = (combine - combine_hi.astype(jnp.float32)).astype(jnp.bfloat16)
    outgoing = jnp.einsum(
        "ts,td->sd", dispatch, post_own, preferred_element_type=jnp.float32
    ).astype(jnp.bfloat16)
    received = lax.all_to_all(
        outgoing.reshape(EXPERTS, capacity, model_width), CHIP_AXES, 0, 0, tiled=True
    )
    piece = received.reshape(slots, model_width)

    def expert_half(gate_up, down):
        gate_part = jnp.dot(piece, gate_up[0], preferred_element_type=jnp.float32)
        up_part = jnp.dot(piece, gate_up[1], preferred_element_type=jnp.float32)
        inner_expert = (jax.nn.silu(gate_part) * up_part).astype(jnp.bfloat16)
        return jnp.dot(inner_expert, down, preferred_element_type=jnp.float32).astype(
            jnp.bfloat16
        )

    summed = (
        expert_half(expert_gate_up[0], expert_down[0]).astype(jnp.float32)
        + expert_half(mate_gate_up[0], mate_down[0]).astype(jnp.float32)
    ).astype(jnp.bfloat16)
    returned = lax.all_to_all(
        summed.reshape(EXPERTS, capacity, model_width), CHIP_AXES, 0, 0, tiled=True
    ).reshape(slots, model_width)
    routed = jnp.dot(combine_hi, returned, preferred_element_type=jnp.float32) + jnp.dot(
        combine_lo, returned, preferred_element_type=jnp.float32
    )
    hidden_out = (residual.astype(jnp.float32) + shared + routed).astype(jnp.bfloat16)
    return (hidden_out, latent_rows, own_rope)


def solution(mesh):
    chip_mesh = Mesh(
        mesh.devices.reshape(mesh.devices.shape[0], -1, 2), ("req",) + HEAD_AXES
    )
    placed = (
        P(("req",) + HEAD_AXES, None),
        P(),
        P(None, HEAD_AXES),
        P(),
        P(),
        P(),
        P(None, HEAD_AXES),
        P(HEAD_AXES, None),
        P("req", None, None),
        P("req", None, None),
        P("req", None),
        P("req"),
        P(),
        P(),
        P(("req",) + HEAD_AXES, None),
        P(None, None, HEAD_AXES),
        P(HEAD_AXES, None),
        P(("req",) + HEAD_AXES, None, None, None),
        P(("req",) + HEAD_AXES, None, None),
    )
    return jax.shard_map(
        body,
        mesh=chip_mesh,
        in_specs=placed,
        out_specs=(P(("req",) + HEAD_AXES, None), P(("req",) + HEAD_AXES, None), P(None, ("req",) + HEAD_AXES)),
        check_vma=False,
    )
```

profile of v0, /device:TPU:32, one launch (start us, length us, event | category | flops | bytes accessed | tf_op | source)
XLA Modules:
  0.0 367.1 jit_solution(14898357139035436531)
XLA Ops:
  9.3 2.0 gather_fusion
  12.9 0.7 copy_bitcast_fusion
  13.6 30.2 %all-gather.4.cloned.1.call-done = bf16[1024,2048]{1,0:T(8,128)(2,1)} async-done(((bf16[128,2048]{1,0:T(8,128)(2,1)}), bf16[1024,2048]{1,0:T(8,128)(2,1)}) %all-gather.4.cloned.1.call-update) | async-done | bytes 4194320 | tf_op jit(solution)/shard_map/all_gather | solution.py:95
  43.8 3.2 fusion.19
  47.3 1.0 fusion.21
  48.7 1.9 fusion.103
  50.6 1.2 copy-done.9
  52.2 2.3 multiply_reduce_fusion
  54.5 0.7 multiply_convert_fusion.3
  55.4 1.1 subtract_convert_fusion.2
  57.3 23.1 %while.12 = (s32[]{:T(128)}, f32[2,1024]{1,0:T(2,128)S(1)}, f32[1024,2,128]{0,2,1:T(8,128)S(1)}, s32[]{:T(128)}, s32[]{:T(128)}, /*index=5*/bf16[2048,512]{1,0:T...) while((s32[]{:T(128)}, f32[2,1024]{1,0:T(2,128)S(1)}, ...), condition=%wide.region_3.4_spmd, body=%wide.region_1.3_spmd.sunk | while | flops 945292288 | bytes 18711784 | solution.py:156
  57.4 1.6 convolution_convert_fusion.6
  58.9 0.8 fusion.149
  60.4 2.1 fusion.150
  63.1 1.6 convolution_convert_fusion.6
  64.7 0.8 fusion.149
  66.1 2.1 fusion.150
  68.9 1.6 convolution_convert_fusion.6
  70.5 0.8 fusion.149
  71.9 2.1 fusion.150
  74.7 1.6 convolution_convert_fusion.6
  76.2 0.8 fusion.149
  77.7 2.1 fusion.150
  80.4 1.4 convolution_bitcast_fusion
  82.0 11.8 %all_gather.14 = bf16[64,1024]{1,0:T(8,128)(2,1)S(1)} all-gather(bf16[64,128]{1,0:T(8,128)(2,1)S(1)} %pad_maximum_fusion.1), channel_id=1, replica_groups=mesh['req'=16,'y'=4,'core'=2] {'y','core'}, dimensions={1}, use_global_device_ids=true | all-gather | bytes 147456 | tf_op jit(solution)/shard_map/all_gather | solution.py:106
  93.7 4.5 %fusion.81 = f32[1024,1024,2]{1,0,2:T(8,128)} fusion(bf16[64,1024]{1,0:T(8,128)(2,1)S(1)} %all_gather.14, bf16[1024,2,32]{0,2,1:T(8,128)(2,1)S(1)} %get-tuple-element.92, bf16[1024,2,32]{0,2,1:T(8,128)(2,1)S(1)} %get-tuple-element.91), kind=kOutput, calls=%fused_computation.105 | convolution fusion | flops 268959744 | bytes 8781824 | tf_op jit(solution)/shard_map/thc,ck->htk/dot_general | solution.py:125
  98.3 2.0 convolution_convert_fusion.4
  100.2 5.2 %fusion.101 = (f32[2,1024]{1,0:T(2,128)S(1)}, bf16[2,1024,1024]{1,2,0:T(8,128)(2,1)S(1)}) fusion(f32[1024,1024,2]{1,0,2:T(8,128)} %fusion.81, bf16[1024,2,256]{0,2,1:T(8,128)(2,1)S(1)} %bitcast.170, pred[1024,1024]{0,1:T(8,128)(4,1)S(1)} %iota_compare_fusion, f32[1024,2,192]{0,2,1:T(8,128)} %bitcast.168), kind=kOutput, calls=%fused_computation.139 | convolution fusion | flops 547354624 | bytes 14688256 | tf_op jit(solution)/shard_map/thc,khc->htk/dot_general | solution.py:120
  105.5 0.7 fusion.61
  106.7 3.2 convolution_convert_fusion.2
  110.0 38.4 %reduce-scatter.3.cloned.1.call-done = bf16[128,2048]{1,0:T(8,128)(2,1)} async-done(((bf16[1024,2048]{1,0:T(8,128)(2,1)}), bf16[128,2048]{1,0:T(8,128)(2,1)}) %reduce-scatter.3.cloned.1.call-update) | async-done | bytes 524304 | tf_op jit(solution)/shard_map/reduce_scatter | solution.py:166
  148.3 1.3 fusion.64
  149.7 2.0 fusion.66
  152.1 1.8 reduce-window.6
  155.1 4.4 %convolution_convert_fusion.3 = bf16[1024,2048]{1,0:T(8,128)(2,1)} fusion(pred[128,1024]{1,0:T(8,128)(4,1)S(1)} %fusion.27, bf16[128,2048]{1,0:T(8,128)(2,1)} %fusion.66), kind=kOutput, calls=%fused_computation.35 | convolution fusion | flops 538968064 | bytes 4849664 | tf_op jit(solution)/shard_map/ts,td->sd/dot_general | solution.py:203
  159.5 8.1 %all-to-all-start = ((bf16[64,16,2048]{2,1,0:T(8,128)(2,1)}), bf16[64,16,2048]{2,1,0:T(8,128)(2,1)}, u32[]{:S(2)}, u32[]{:S(2)}) async-start(bf16[64,16,2048]{2,1,0:T(8,128)(2,1)} %bitcast.162), calls=%async_computation.2 | async-start | bytes 8388608 | tf_op jit(solution)/shard_map/all_to_all | solution.py:206
  168.4 61.2 %all-to-all-done = bf16[64,16,2048]{2,1,0:T(8,128)(2,1)} async-done(((bf16[64,16,2048]{2,1,0:T(8,128)(2,1)}), bf16[64,16,2048]{2,1,0:T(8,128)(2,1)}, u32[]{:S(2)}, u32[]{:S(2)}) %all-to-all-start) | async-done | bytes 4194336 | tf_op jit(solution)/shard_map/all_to_all | solution.py:206
  229.6 7.9 %fusion.33 = f32[1024,704]{0,1:T(8,128)} fusion(bf16[1024,2048]{1,0:T(8,128)(2,1)} %bitcast.22, bf16[1,2,2048,704]{2,3,1,0:T(8,128)(2,1)} %param.38), kind=kOutput, calls=%fused_computation.46 | convolution fusion | flops 2952790016 | bytes 9961472 | tf_op jit(solution)/shard_map/dot_general | solution.py:213
  237.5 5.5 %fusion.44 = f32[1024,352]{0,1:T(8,128)} fusion(bf16[1024,2048]{1,0:T(8,128)(2,1)} %all-gather.8.cloned.1.call-done, bf16[2,2048,352]{1,2,0:T(8,128)(2,1)} %param.36), kind=kOutput, calls=%fused_computation.63 | convolution fusion | flops 1476395008 | bytes 7077888 | tf_op jit(solution)/shard_map/dot_general | solution.py:175
  243.0 9.5 %convolution_convert_fusion.1 = bf16[1024,2048]{1,0:T(8,128)(2,1)} fusion(bf16[352,2048]{1,0:T(8,128)(2,1)} %param.37, bf16[1024,2048]{1,0:T(8,128)(2,1)} %all-gather.8.cloned.1.call-done, bf16[2,2048,352]{1,2,0:T(8,128)(2,1)} %param.36, f32[1024,352]{0,1:T(8,128)} %fusion.44), kind=kOutput, calls=%fused_computation.33 | convolution fusion | flops 2957049856 | bytes 12713984 | tf_op jit(solution)/shard_map/dot_general | solution.py:180
  252.5 7.9 %fusion.28 = f32[1024,704]{0,1:T(8,128)} fusion(bf16[1024,2048]{1,0:T(8,128)(2,1)} %bitcast.22, bf16[1,2,2048,704]{2,3,1,0:T(8,128)(2,1)} %collective-permute-done), kind=kOutput, calls=%fused_computation.40 | convolution fusion | flops 2952790016 | bytes 9961472 | tf_op jit(solution)/shard_map/dot_general | solution.py:213
  260.4 12.7 %fusion.31 = bf16[1024,2048]{1,0:T(8,128)(2,1)} fusion(bf16[1,704,2048]{2,1,0:T(8,128)(2,1)} %param.39, f32[1024,704]{0,1:T(8,128)} %fusion.33, bf16[1024,2048]{1,0:T(8,128)(2,1)} %bitcast.22, bf16[1,2,2048,704]{2,3,1,0:T(8,128)(2,1)} %param.38), kind=kOutput, calls=%fused_computation.44 | convolution fusion | flops 5909905408 | bytes 17039360 | tf_op jit(solution)/shard_map/dot_general | solution.py:215
  273.1 13.5 %add_convert_fusion = bf16[1024,2048]{1,0:T(8,128)(2,1)} fusion(bf16[1024,2048]{1,0:T(8,128)(2,1)} %fusion.31, bf16[1,704,2048]{2,1,0:T(8,128)(2,1)} %collective-permute-done.1, f32[1024,704]{0,1:T(8,128)} %fusion.28, bf16[1024,2048]{1,0:T(8,128)(2,1)} %bitcast.22, bf16[1,2,2048,704]{2,3,1,0:T(8,128)(2,1)} %collective-permute-done), kind=kOutput, calls=%fused_computation.29 | convolution fusion | flops 5920391168 | bytes 21233664 | tf_op jit(solution)/shard_map/dot_general | solution.py:215
  286.6 9.2 %all-to-all-start.1 = ((bf16[64,16,2048]{2,1,0:T(8,128)(2,1)}), bf16[64,16,2048]{2,1,0:T(8,128)(2,1)}, u32[]{:S(2)}, u32[]{:S(2)}) async-start(bf16[64,16,2048]{2,1,0:T(8,128)(2,1)} %bitcast.164), calls=%async_computation.3 | async-start | bytes 8388608 | tf_op jit(solution)/shard_map/all_to_all | solution.py:223
  296.1 1.2 select_reduce_fusion
  297.4 54.2 %all-to-all-done.1 = bf16[64,16,2048]{2,1,0:T(8,128)(2,1)} async-done(((bf16[64,16,2048]{2,1,0:T(8,128)(2,1)}), bf16[64,16,2048]{2,1,0:T(8,128)(2,1)}, u32[]{:S(2)}, u32[]{:S(2)}) %all-to-all-start.1) | async-done | bytes 4194336 | tf_op jit(solution)/shard_map/all_to_all | solution.py:223
  351.6 4.2 %fusion.84 = f32[128,2048]{1,0:T(8,128)} fusion(bf16[1024,2048]{1,0:T(8,128)(2,1)} %bitcast.30, f32[128,1024]{1,0:T(8,128)} %select_reduce_fusion), kind=kOutput, calls=%fused_computation.108 | convolution fusion | flops 537001984 | bytes 5767168 | tf_op jit(solution)/shard_map/dot_general | solution.py:226
  355.8 4.6 %fusion.40 = bf16[128,2048]{1,0:T(8,128)(2,1)} fusion(f32[128,2048]{1,0:T(8,128)} %fusion.84, bf16[1024,2048]{1,0:T(8,128)(2,1)} %bitcast.30, bf16[128,2048]{1,0:T(8,128)(2,1)} %reduce-scatter.5.cloned.1.call-done, f32[128,1024]{1,0:T(8,128)} %select_reduce_fusion, bf16[128,2048]{1,0:T(8,128)(2,1)S(1)} %copy-done.7, bf16[128,2048]{1,0:T(8,128)(2,1)S(1)} %copy-done.5), kind=kOutput, calls=%fused_computation.56 | convolution fusion | flops 540016640 | bytes 7864320 | tf_op jit(solution)/shard_map/dot_general | solution.py:226
  (106 shorter events, 13.2 us)
Async XLA Ops:
  7.2 2.1 copy-start
  7.2 4.1 %copy-start.11 = (bf16[16,64,128]{2,1,0:T(8,128)(2,1)S(1)}, bf16[16,64,128]{2,1,0:T(8,128)(2,1)}, u32[]{:S(2)}) copy-start(bf16[16,64,128]{2,1,0:T(8,128)(2,1)} %param.30) | copy-start | bytes 786436
  7.2 36.6 %all-gather.4.cloned.1.call-start = ((), (), s32[]{:S(2)}) async-start(), calls=%async_computation.4 | async-start | bytes 4718592 | tf_op jit(solution)/shard_map/all_gather | solution.py:95
  7.9 90.3 %all-gather.6.cloned.1.call-start = ((), (), s32[]{:S(2)}) async-start(), calls=%async_computation.5 | async-start | bytes 1179648 | tf_op jit(solution)/shard_map/all_gather | solution.py:105
  11.3 35.8 %copy-start.15 = (f32[2048]{0:T(1024)S(1)}, f32[2048]{0:T(1024)}, u32[]{:S(2)}) copy-start(f32[2048]{0:T(1024)} %param.22) | copy-start | bytes 24580
  43.8 3.4 copy-start.2
  47.3 1.4 copy-start.18
  48.7 1.9 copy-start.6
  50.6 1.2 copy-start.9
  50.6 3.9 %copy-start.17 = (f32[512]{0:T(512)S(1)}, f32[512]{0:T(512)}, u32[]{:S(2)}) copy-start(f32[512]{0:T(512)} %param.26) | copy-start | bytes 6148
  50.6 6.7 %copy-start.3 = (bf16[512,512]{1,0:T(8,128)(2,1)S(1)}, bf16[512,512]{1,0:T(8,128)(2,1)}, u32[]{:S(2)}) copy-start(bf16[512,512]{1,0:T(8,128)(2,1)} %param.27) | copy-start | bytes 1572868
  55.3 93.0 %reduce-scatter.3.cloned.1.call-start = ((), (), s32[]{:S(2)}) async-start(), calls=%async_computation.6 | async-start | bytes 4718592 | tf_op jit(solution)/shard_map/reduce_scatter | solution.py:166
  57.4 3.0 copy-start.12
  63.1 3.0 copy-start.12
  68.9 3.0 copy-start.12
  74.6 3.0 copy-start.12
  82.0 16.3 %copy-start.13 = (bf16[64,128]{1,0:T(8,128)(2,1)}, bf16[64,128]{1,0:T(8,128)(2,1)S(1)}, u32[]{:S(2)}) copy-start(bf16[64,128]{1,0:T(8,128)(2,1)S(1)} %pad_maximum_fusion.1) | copy-start | bytes 49156
  105.4 1.2 copy-start.8
  106.7 41.7 %copy-start.5 = (bf16[128,2048]{1,0:T(8,128)(2,1)S(1)}, bf16[128,2048]{1,0:T(8,128)(2,1)}, u32[]{:S(2)}) copy-start(bf16[128,2048]{1,0:T(8,128)(2,1)} %param.21) | copy-start | bytes 1572868
  109.9 39.7 %copy-start.16 = (f32[2048]{0:T(1024)S(1)}, f32[2048]{0:T(1024)}, u32[]{:S(2)}) copy-start(f32[2048]{0:T(1024)} %param.33) | copy-start | bytes 24580
  109.9 41.8 %copy-start.14 = (s32[128,6]{0,1:T(8,128)S(1)}, s32[128,6]{0,1:T(8,128)}, u32[]{:S(2)}) copy-start(s32[128,6]{0,1:T(8,128)} %param.35) | copy-start | bytes 9220
  109.9 127.5 %all-gather.8.cloned.1.call-start = ((), (), s32[]{:S(2)}) async-start(), calls=%async_computation.7 | async-start | bytes 4718592 | tf_op jit(solution)/shard_map/all_gather | solution.py:174
  159.5 70.1 %all-to-all-start = ((bf16[64,16,2048]{2,1,0:T(8,128)(2,1)}), bf16[64,16,2048]{2,1,0:T(8,128)(2,1)}, u32[]{:S(2)}, u32[]{:S(2)}) async-start(bf16[64,16,2048]{2,1,0:T(8,128)(2,1)} %bitcast.162), calls=%async_computation.2 | async-start | bytes 8388608 | tf_op jit(solution)/shard_map/all_to_all | solution.py:206
  167.6 188.1 %reduce-scatter.5.cloned.1.call-start = ((), (), s32[]{:S(2)}) async-start(), calls=%async_computation.8 | async-start | bytes 4718592 | tf_op jit(solution)/shard_map/reduce_scatter | solution.py:179
  167.7 84.8 %collective-permute-start = (bf16[1,2,2048,704]{2,3,1,0:T(8,128)(2,1)}, bf16[1,2,2048,704]{2,3,1,0:T(8,128)(2,1)}, u32[]{:S(2)}, u32[]{:S(2)}) collective-permute-start(bf16[1,2,2048,704]{2,3,1,0:T(8,128)(2,1)} %param.38), channel_id=1, source_target_pairs={{0,1},{1,0},{2,3},{3,2},{4,5},{5,4},{6,7},{7,6},{8,9},{9,8},{10,11... | collective-permute-start | bytes 17301512 | tf_op jit(solution)/shard_map/ppermute | solution.py:81
  167.8 105.3 %collective-permute-start.1 = (bf16[1,704,2048]{2,1,0:T(8,128)(2,1)}, bf16[1,704,2048]{2,1,0:T(8,128)(2,1)}, u32[]{:S(2)}, u32[]{:S(2)}) collective-permute-start(bf16[1,704,2048]{2,1,0:T(8,128)(2,1)} %param.39), channel_id=1, source_target_pairs={{0,1},{1,0},{2,3},{3,2},{4,5},{5,4},{6,7},{7,6},{8,9},{9,8},{10,11... | collective-permute-start | bytes 8650760 | tf_op jit(solution)/shard_map/ppermute | solution.py:82
  286.5 9.2 %copy-start.4 = (bf16[128,2048]{1,0:T(8,128)(2,1)S(1)}, bf16[128,2048]{1,0:T(8,128)(2,1)}, u32[]{:S(2)}) copy-start(bf16[128,2048]{1,0:T(8,128)(2,1)} %fusion.66) | copy-start | bytes 1572868
  286.6 9.2 %copy-start.10 = (bf16[2048,64]{0,1:T(8,128)(2,1)S(1)}, bf16[2048,64]{0,1:T(8,128)(2,1)}, u32[]{:S(2)}) copy-start(bf16[2048,64]{0,1:T(8,128)(2,1)} %param.34) | copy-start | bytes 786436
  286.6 65.0 %all-to-all-start.1 = ((bf16[64,16,2048]{2,1,0:T(8,128)(2,1)}), bf16[64,16,2048]{2,1,0:T(8,128)(2,1)}, u32[]{:S(2)}, u32[]{:S(2)}) async-start(bf16[64,16,2048]{2,1,0:T(8,128)(2,1)} %bitcast.164), calls=%async_computation.3 | async-start | bytes 8388608 | tf_op jit(solution)/shard_map/all_to_all | solution.py:223
  295.8 60.0 %copy-start.7 = (bf16[128,2048]{1,0:T(8,128)(2,1)S(1)}, bf16[128,2048]{1,0:T(8,128)(2,1)}, u32[]{:S(2)}) copy-start(bf16[128,2048]{1,0:T(8,128)(2,1)} %reduce-scatter.3.cloned.1.call-done) | copy-start | bytes 1572868
  351.6 8.8 %copy-start.1 = (bf16[16,128,512]{2,1,0:T(8,128)(2,1)S(1)}, bf16[16,128,512]{2,1,0:T(8,128)(2,1)}, u32[]{:S(2)}) copy-start(bf16[16,128,512]{2,1,0:T(8,128)(2,1)} %param.29) | copy-start | bytes 6291460
Sparse Core Ops, SparseCore 0:
  9.7 34.0 all-gather.3
  55.4 23.1 all-gather.5
  110.0 38.2 reduce-scatter.2
  151.8 74.8 all-gather.7
  252.6 38.1 reduce-scatter.4
where the time goes:
time: 375 us; the launch traced here: 367 us
  waiting for transfers between devices  185 us (49%)
  matrix products  112 us (30%)
  other arithmetic  18.3 us (5%)
  starting transfers between devices  18.2 us (5%)
  between operations  15.1 us (4%)
  blocking collectives  11.8 us (3%)
  local copies, waits for them, and re-layouts  7.09 us (2%)
    all_to_all x1, waiting for transfers between devices, body(): lax.all_to_all(outgoing.reshape(EXPERTS, capacity, model_width), CHIP_AXE...  61.2 us
    all_to_all x1, waiting for transfers between devices, body(): lax.all_to_all(summed.reshape(EXPERTS, capacity, model_width), CHIP_AXES,...  54.2 us
    reduce_scatter x1, waiting for transfers between devices, body(): lax.psum_scatter(jnp.dot(rows_block, out_weight, preferred_element_type=j...  38.4 us
    all_gather x1, waiting for transfers between devices, body(): gathered = lax.all_gather(hidden_in, HEAD_AXES, axis=0, tiled=True)  30.2 us
    dot_general x2, matrix products, expert_half(): jnp.dot(inner_expert, down, preferred_element_type=jnp.float32)  26.2 us
    dot_general x2, matrix products, expert_half(): up_part = jnp.dot(piece, gate_up[1], preferred_element_type=jnp.float32)  15.8 us
    dot_general x5, matrix products, score_block(): jnp.einsum('thc,ck->htk', query_rope, keys_rope, preferred_element_type=j...  13 us
    all_gather x1, blocking collectives, body(): lax.all_gather(own_rope, HEAD_AXES, axis=1, tiled=True)  11.8 us
  transfers between devices with their start and end apart: 9, of which 4 were waited for; matrix products, arithmetic and copies ran while one was open for 29% of the time, Pallas kernels for 0%

commit v1 on v0

--- a/solution.py
+++ b/solution.py
@@ -162,13 +162,21 @@
         .astype(jnp.bfloat16)
         .reshape(fresh_count, local_heads * VDIM)
     )
-    rows_block = attended
-    attn_sum = lax.psum_scatter(
-        jnp.dot(rows_block, out_weight, preferred_element_type=jnp.float32).astype(jnp.bfloat16),
-        HEAD_AXES,
-        scatter_dimension=0,
-        tiled=True,
-    ).astype(jnp.float32)
+    chip_count = lax.axis_size("y")
+    core_count = lax.axis_size("core")
+    rows_block = jnp.transpose(
+        attended.reshape(chip_count, core_count, own_rows, local_heads * VDIM), (1, 0, 2, 3)
+    ).reshape(fresh_count, local_heads * VDIM)
+    partial = jnp.dot(rows_block, out_weight, preferred_element_type=jnp.float32).astype(
+        jnp.bfloat16
+    )
+    core_parts = lax.all_to_all(
+        partial.reshape(core_count, chip_count * own_rows, model_width), "core", 0, 0, tiled=True
+    )
+    chip_part = jnp.sum(core_parts.astype(jnp.float32), axis=0).astype(jnp.bfloat16)
+    attn_sum = lax.psum_scatter(chip_part, "y", scatter_dimension=0, tiled=True).astype(
+        jnp.float32
+    )
     residual = (hidden_in.astype(jnp.float32) + attn_sum).astype(jnp.bfloat16)
     post_own = rms_norm(residual, post_gain).astype(jnp.bfloat16)
     piece = lax.all_gather(post_own, HEAD_AXES, axis=0, tiled=True)

time: 375 us -> 378 us (level)
  waiting for transfers between devices: 185 us -> 176 us
  blocking collectives: 11.8 us -> 19.9 us
  other arithmetic: 18.3 us -> 23.4 us
    reduce_scatter x1, waiting for transfers between devices: 38.4 us -> 30.2 us  [body(): lax.psum_scatter(chip_part, 'y', scatter_dimension=0, tiled=True)]
    all_to_all x0 -> x1, blocking collectives: none -> 8.17 us  [body(): lax.all_to_all(partial.reshape(core_count, chip_count * own_rows, model_w...]
    reduce_sum x0 -> x1, other arithmetic: none -> 5.09 us  [body(): jnp.sum(core_parts.astype(jnp.float32), axis=0).astype(jnp.bfloat16)]
where the time goes in v1:
time: 378 us; the launch traced here: 371 us
  waiting for transfers between devices  176 us (47%)
  matrix products  110 us (29%)
  other arithmetic  23.4 us (6%)
  blocking collectives  19.9 us (5%)
  starting transfers between devices  19 us (5%)
  between operations  15.1 us (4%)
  local copies, waits for them, and re-layouts  7.54 us (2%)
    all_to_all x1, waiting for transfers between devices, body(): lax.all_to_all(outgoing.reshape(EXPERTS, capacity, model_width), CHIP_AXE...  61.6 us
    all_to_all x1, waiting for transfers between devices, body(): lax.all_to_all(summed.reshape(EXPERTS, capacity, model_width), CHIP_AXES,...  53.3 us
    reduce_scatter x1, waiting for transfers between devices, body(): lax.psum_scatter(chip_part, 'y', scatter_dimension=0, tiled=True)  30.2 us
    all_gather x1, waiting for transfers between devices, body(): gathered = lax.all_gather(hidden_in, HEAD_AXES, axis=0, tiled=True)  30.2 us
    dot_general x2, matrix products, expert_half(): jnp.dot(inner_expert, down, preferred_element_type=jnp.float32)  26.1 us
    dot_general x2, matrix products, expert_half(): up_part = jnp.dot(piece, gate_up[1], preferred_element_type=jnp.float32)  15.8 us
    dot_general x5, matrix products, score_block(): jnp.einsum('thc,ck->htk', query_rope, keys_rope, preferred_element_type=j...  13 us
    all_gather x1, blocking collectives, body(): lax.all_gather(own_rope, HEAD_AXES, axis=1, tiled=True)  11.8 us
  transfers between devices with their start and end apart: 9, of which 4 were waited for; matrix products, arithmetic and copies ran while one was open for 29% of the time, Pallas kernels for 0%

profile of v1, /device:TPU:32, one launch (start us, length us, event | category | flops | bytes accessed | tf_op | source)
XLA Modules:
  0.0 370.9 jit_solution(13068889929089673657)
XLA Ops:
  9.3 2.0 gather_fusion
  13.7 30.2 %all-gather.4.cloned.1.call-done = bf16[1024,2048]{1,0:T(8,128)(2,1)} async-done(((bf16[128,2048]{1,0:T(8,128)(2,1)}), bf16[1024,2048]{1,0:T(8,128)(2,1)}) %all-gather.4.cloned.1.call-update) | async-done | bytes 4194320 | tf_op jit(solution)/shard_map/all_gather | solution.py:95
  43.8 3.2 fusion.19
  47.3 1.0 fusion.21
  48.7 1.9 fusion.103
  50.6 1.2 copy-done.9
  52.2 2.3 multiply_reduce_fusion
  54.5 0.7 multiply_convert_fusion.3
  55.4 1.1 subtract_convert_fusion.2
  57.3 23.0 %while.12 = (s32[]{:T(128)}, f32[2,1024]{1,0:T(2,128)S(1)}, f32[1024,2,128]{0,2,1:T(8,128)S(1)}, s32[]{:T(128)}, s32[]{:T(128)}, /*index=5*/bf16[2048,512]{1,0:T...) while((s32[]{:T(128)}, f32[2,1024]{1,0:T(2,128)S(1)}, ...), condition=%wide.region_3.4_spmd, body=%wide.region_1.3_spmd.sunk | while | flops 945292288 | bytes 18711784 | solution.py:156
  57.4 1.6 convolution_convert_fusion.6
  58.9 0.8 fusion.149
  60.4 2.1 fusion.150
  63.1 1.6 convolution_convert_fusion.6
  64.7 0.8 fusion.149
  66.1 2.1 fusion.150
  68.9 1.6 convolution_convert_fusion.6
  70.5 0.8 fusion.149
  71.9 2.1 fusion.150
  74.6 1.6 convolution_convert_fusion.6
  76.2 0.8 fusion.149
  77.7 2.1 fusion.150
  80.4 1.4 convolution_bitcast_fusion
  82.0 11.8 %all_gather.14 = bf16[64,1024]{1,0:T(8,128)(2,1)S(1)} all-gather(bf16[64,128]{1,0:T(8,128)(2,1)S(1)} %pad_maximum_fusion.1), channel_id=1, replica_groups=mesh['req'=16,'y'=4,'core'=2] {'y','core'}, dimensions={1}, use_global_device_ids=true | all-gather | bytes 147456 | tf_op jit(solution)/shard_map/all_gather | solution.py:106
  93.7 4.5 %fusion.81 = f32[1024,1024,2]{1,0,2:T(8,128)} fusion(bf16[64,1024]{1,0:T(8,128)(2,1)S(1)} %all_gather.14, bf16[1024,2,32]{0,2,1:T(8,128)(2,1)S(1)} %get-tuple-element.92, bf16[1024,2,32]{0,2,1:T(8,128)(2,1)S(1)} %get-tuple-element.91), kind=kOutput, calls=%fused_computation.105 | convolution fusion | flops 268959744 | bytes 8781824 | tf_op jit(solution)/shard_map/thc,ck->htk/dot_general | solution.py:125
  98.2 2.0 convolution_convert_fusion.4
  100.2 5.2 %fusion.101 = (f32[2,1024]{1,0:T(2,128)S(1)}, bf16[2,1024,1024]{1,2,0:T(8,128)(2,1)S(1)}) fusion(f32[1024,1024,2]{1,0,2:T(8,128)} %fusion.81, bf16[1024,2,256]{0,2,1:T(8,128)(2,1)S(1)} %bitcast.176, pred[1024,1024]{0,1:T(8,128)(4,1)S(1)} %iota_compare_fusion, f32[1024,2,192]{0,2,1:T(8,128)} %bitcast.174), kind=kOutput, calls=%fused_computation.139 | convolution fusion | flops 547354624 | bytes 14688256 | tf_op jit(solution)/shard_map/thc,khc->htk/dot_general | solution.py:120
  107.1 1.3 convolution_convert_fusion.2
  108.4 8.2 %all_to_all.15 = bf16[2,512,2048]{2,1,0:T(8,128)(2,1)} all-to-all(bf16[2,512,2048]{2,1,0:T(8,128)(2,1)S(1)} %bitcast.168), channel_id=1, replica_groups=mesh['req'=16,'y'=4,'core'=2] {'core'}, dimensions={0} | all-to-all | bytes 8388608 | tf_op jit(solution)/shard_map/all_to_all | solution.py:173
  116.6 5.1 %reduce_sum.98 = bf16[512,2048]{1,0:T(8,128)(2,1)} reduce(bf16[2,512,2048]{2,1,0:T(8,128)(2,1)} %all_to_all.15, bf16[]{:T(256)} %constant.86.clone.1), dimensions={0}, to_apply=%region_6.7 | reduce | flops 1048576 | bytes 6291458 | tf_op jit(solution)/shard_map/reduce_sum | solution.py:176
  121.7 30.2 %reduce-scatter.3.cloned.1.call-done = bf16[128,2048]{1,0:T(8,128)(2,1)} async-done(((bf16[512,2048]{1,0:T(8,128)(2,1)}), bf16[128,2048]{1,0:T(8,128)(2,1)}) %reduce-scatter.3.cloned.1.call-update) | async-done | bytes 524304 | tf_op jit(solution)/shard_map/reduce_scatter | solution.py:177
  151.9 1.3 fusion.64
  153.2 2.0 fusion.66
  155.7 1.8 reduce-window.6
  158.7 4.4 %convolution_convert_fusion.3 = bf16[1024,2048]{1,0:T(8,128)(2,1)} fusion(pred[128,1024]{1,0:T(8,128)(4,1)S(1)} %fusion.27, bf16[128,2048]{1,0:T(8,128)(2,1)} %fusion.66), kind=kOutput, calls=%fused_computation.35 | convolution fusion | flops 538968064 | bytes 4849664 | tf_op jit(solution)/shard_map/ts,td->sd/dot_general | solution.py:211
  163.0 9.0 %all-to-all-start.1 = ((bf16[64,16,2048]{2,1,0:T(8,128)(2,1)}), bf16[64,16,2048]{2,1,0:T(8,128)(2,1)}, u32[]{:S(2)}, u32[]{:S(2)}) async-start(bf16[64,16,2048]{2,1,0:T(8,128)(2,1)} %bitcast.167), calls=%async_computation.3 | async-start | bytes 8388608 | tf_op jit(solution)/shard_map/all_to_all | solution.py:214
  172.8 61.6 %all-to-all-done.1 = bf16[64,16,2048]{2,1,0:T(8,128)(2,1)} async-done(((bf16[64,16,2048]{2,1,0:T(8,128)(2,1)}), bf16[64,16,2048]{2,1,0:T(8,128)(2,1)}, u32[]{:S(2)}, u32[]{:S(2)}) %all-to-all-start.1) | async-done | bytes 4194336 | tf_op jit(solution)/shard_map/all_to_all | solution.py:214
  234.4 7.9 %fusion.33 = f32[1024,704]{0,1:T(8,128)} fusion(bf16[1024,2048]{1,0:T(8,128)(2,1)} %bitcast.24, bf16[1,2,2048,704]{2,3,1,0:T(8,128)(2,1)} %param.38), kind=kOutput, calls=%fused_computation.46 | convolution fusion | flops 2952790016 | bytes 9961472 | tf_op jit(solution)/shard_map/dot_general | solution.py:221
  242.3 5.5 %fusion.44 = f32[1024,352]{0,1:T(8,128)} fusion(bf16[1024,2048]{1,0:T(8,128)(2,1)} %all-gather.8.cloned.1.call-done, bf16[2,2048,352]{1,2,0:T(8,128)(2,1)} %param.36), kind=kOutput, calls=%fused_computation.63 | convolution fusion | flops 1476395008 | bytes 7077888 | tf_op jit(solution)/shard_map/dot_general | solution.py:183
  247.7 9.5 %convolution_convert_fusion.1 = bf16[1024,2048]{1,0:T(8,128)(2,1)} fusion(bf16[352,2048]{1,0:T(8,128)(2,1)} %param.37, bf16[1024,2048]{1,0:T(8,128)(2,1)} %all-gather.8.cloned.1.call-done, bf16[2,2048,352]{1,2,0:T(8,128)(2,1)} %param.36, f32[1024,352]{0,1:T(8,128)} %fusion.44), kind=kOutput, calls=%fused_computation.33 | convolution fusion | flops 2957049856 | bytes 12713984 | tf_op jit(solution)/shard_map/dot_general | solution.py:188
  257.2 7.9 %fusion.28 = f32[1024,704]{0,1:T(8,128)} fusion(bf16[1024,2048]{1,0:T(8,128)(2,1)} %bitcast.24, bf16[1,2,2048,704]{2,3,1,0:T(8,128)(2,1)} %collective-permute-done), kind=kOutput, calls=%fused_computation.40 | convolution fusion | flops 2952790016 | bytes 9961472 | tf_op jit(solution)/shard_map/dot_general | solution.py:221
  265.1 12.7 %fusion.31 = bf16[1024,2048]{1,0:T(8,128)(2,1)} fusion(bf16[1,704,2048]{2,1,0:T(8,128)(2,1)} %param.39, f32[1024,704]{0,1:T(8,128)} %fusion.33, bf16[1024,2048]{1,0:T(8,128)(2,1)} %bitcast.24, bf16[1,2,2048,704]{2,3,1,0:T(8,128)(2,1)} %param.38), kind=kOutput, calls=%fused_computation.44 | convolution fusion | flops 5909905408 | bytes 17039360 | tf_op jit(solution)/shard_map/dot_general | solution.py:223
  277.8 13.4 %add_convert_fusion = bf16[1024,2048]{1,0:T(8,128)(2,1)} fusion(bf16[1024,2048]{1,0:T(8,128)(2,1)} %fusion.31, bf16[1,704,2048]{2,1,0:T(8,128)(2,1)} %collective-permute-done.1, f32[1024,704]{0,1:T(8,128)} %fusion.28, bf16[1024,2048]{1,0:T(8,128)(2,1)} %bitcast.24, bf16[1,2,2048,704]{2,3,1,0:T(8,128)(2,1)} %collective-permute-done), kind=kOutput, calls=%fused_computation.29 | convolution fusion | flops 5920391168 | bytes 21233664 | tf_op jit(solution)/shard_map/dot_general | solution.py:223
  291.2 9.2 %all-to-all-start.2 = ((bf16[64,16,2048]{2,1,0:T(8,128)(2,1)}), bf16[64,16,2048]{2,1,0:T(8,128)(2,1)}, u32[]{:S(2)}, u32[]{:S(2)}) async-start(bf16[64,16,2048]{2,1,0:T(8,128)(2,1)} %bitcast.170), calls=%async_computation.4 | async-start | bytes 8388608 | tf_op jit(solution)/shard_map/all_to_all | solution.py:231
  300.8 1.2 select_reduce_fusion
  302.0 53.3 %all-to-all-done.2 = bf16[64,16,2048]{2,1,0:T(8,128)(2,1)} async-done(((bf16[64,16,2048]{2,1,0:T(8,128)(2,1)}), bf16[64,16,2048]{2,1,0:T(8,128)(2,1)}, u32[]{:S(2)}, u32[]{:S(2)}) %all-to-all-start.2) | async-done | bytes 4194336 | tf_op jit(solution)/shard_map/all_to_all | solution.py:231
  355.4 4.2 %fusion.84 = f32[128,2048]{1,0:T(8,128)} fusion(bf16[1024,2048]{1,0:T(8,128)(2,1)} %bitcast.32, f32[128,1024]{1,0:T(8,128)} %select_reduce_fusion), kind=kOutput, calls=%fused_computation.108 | convolution fusion | flops 537001984 | bytes 5767168 | tf_op jit(solution)/shard_map/dot_general | solution.py:234
  359.5 4.6 %fusion.40 = bf16[128,2048]{1,0:T(8,128)(2,1)} fusion(f32[128,2048]{1,0:T(8,128)} %fusion.84, bf16[1024,2048]{1,0:T(8,128)(2,1)} %bitcast.32, bf16[128,2048]{1,0:T(8,128)(2,1)} %reduce-scatter.5.cloned.1.call-done, f32[128,1024]{1,0:T(8,128)} %select_reduce_fusion, bf16[128,2048]{1,0:T(8,128)(2,1)S(1)} %copy-done.7, bf16[128,2048]{1,0:T(8,128)(2,1)S(1)} %copy-done.5), kind=kOutput, calls=%fused_computation.56 | convolution fusion | flops 540016640 | bytes 7864320 | tf_op jit(solution)/shard_map/dot_general | solution.py:234
  (110 shorter events, 15.1 us)
Async XLA Ops:
  7.2 2.1 copy-start
  7.2 4.1 %copy-start.11 = (bf16[16,64,128]{2,1,0:T(8,128)(2,1)S(1)}, bf16[16,64,128]{2,1,0:T(8,128)(2,1)}, u32[]{:S(2)}) copy-start(bf16[16,64,128]{2,1,0:T(8,128)(2,1)} %param.30) | copy-start | bytes 786436
  7.2 36.6 %all-gather.4.cloned.1.call-start = ((), (), s32[]{:S(2)}) async-start(), calls=%async_computation.5 | async-start | bytes 4718592 | tf_op jit(solution)/shard_map/all_gather | solution.py:95
  7.9 90.3 %all-gather.6.cloned.1.call-start = ((), (), s32[]{:S(2)}) async-start(), calls=%async_computation.6 | async-start | bytes 1179648 | tf_op jit(solution)/shard_map/all_gather | solution.py:105
  11.3 35.7 %copy-start.15 = (f32[2048]{0:T(1024)S(1)}, f32[2048]{0:T(1024)}, u32[]{:S(2)}) copy-start(f32[2048]{0:T(1024)} %param.22) | copy-start | bytes 24580
  43.8 3.4 copy-start.2
  47.3 1.4 copy-start.18
  48.7 1.9 copy-start.6
  50.6 1.2 copy-start.9
  50.6 3.9 %copy-start.17 = (f32[512]{0:T(512)S(1)}, f32[512]{0:T(512)}, u32[]{:S(2)}) copy-start(f32[512]{0:T(512)} %param.26) | copy-start | bytes 6148
  50.6 6.7 %copy-start.3 = (bf16[512,512]{1,0:T(8,128)(2,1)S(1)}, bf16[512,512]{1,0:T(8,128)(2,1)}, u32[]{:S(2)}) copy-start(bf16[512,512]{1,0:T(8,128)(2,1)} %param.27) | copy-start | bytes 1572868
  55.3 96.6 %reduce-scatter.3.cloned.1.call-start = ((), (), s32[]{:S(2)}) async-start(), calls=%async_computation.7 | async-start | bytes 2621440 | tf_op jit(solution)/shard_map/reduce_scatter | solution.py:177
  57.3 3.0 copy-start.12
  63.1 3.0 copy-start.12
  68.9 3.0 copy-start.12
  74.6 3.0 copy-start.12
  82.0 16.3 %copy-start.13 = (bf16[64,128]{1,0:T(8,128)(2,1)}, bf16[64,128]{1,0:T(8,128)(2,1)S(1)}, u32[]{:S(2)}) copy-start(bf16[64,128]{1,0:T(8,128)(2,1)S(1)} %pad_maximum_fusion.1) | copy-start | bytes 49156
  105.4 1.7 copy-start.8
  116.6 35.4 %copy-start.5 = (bf16[128,2048]{1,0:T(8,128)(2,1)S(1)}, bf16[128,2048]{1,0:T(8,128)(2,1)}, u32[]{:S(2)}) copy-start(bf16[128,2048]{1,0:T(8,128)(2,1)} %param.21) | copy-start | bytes 1572868
  116.6 36.7 %copy-start.16 = (f32[2048]{0:T(1024)S(1)}, f32[2048]{0:T(1024)}, u32[]{:S(2)}) copy-start(f32[2048]{0:T(1024)} %param.33) | copy-start | bytes 24580
  121.6 33.6 %copy-start.14 = (s32[128,6]{0,1:T(8,128)S(1)}, s32[128,6]{0,1:T(8,128)}, u32[]{:S(2)}) copy-start(s32[128,6]{0,1:T(8,128)} %param.35) | copy-start | bytes 9220
  121.7 120.6 %all-gather.8.cloned.1.call-start = ((), (), s32[]{:S(2)}) async-start(), calls=%async_computation.8 | async-start | bytes 4718592 | tf_op jit(solution)/shard_map/all_gather | solution.py:182
  163.0 71.3 %all-to-all-start.1 = ((bf16[64,16,2048]{2,1,0:T(8,128)(2,1)}), bf16[64,16,2048]{2,1,0:T(8,128)(2,1)}, u32[]{:S(2)}, u32[]{:S(2)}) async-start(bf16[64,16,2048]{2,1,0:T(8,128)(2,1)} %bitcast.167), calls=%async_computation.3 | async-start | bytes 8388608 | tf_op jit(solution)/shard_map/all_to_all | solution.py:214
  172.0 187.5 %reduce-scatter.5.cloned.1.call-start = ((), (), s32[]{:S(2)}) async-start(), calls=%async_computation.9 | async-start | bytes 4718592 | tf_op jit(solution)/shard_map/reduce_scatter | solution.py:187
  172.1 85.2 %collective-permute-start = (bf16[1,2,2048,704]{2,3,1,0:T(8,128)(2,1)}, bf16[1,2,2048,704]{2,3,1,0:T(8,128)(2,1)}, u32[]{:S(2)}, u32[]{:S(2)}) collective-permute-start(bf16[1,2,2048,704]{2,3,1,0:T(8,128)(2,1)} %param.38), channel_id=1, source_target_pairs={{0,1},{1,0},{2,3},{3,2},{4,5},{5,4},{6,7},{7,6},{8,9},{9,8},{10,11... | collective-permute-start | bytes 17301512 | tf_op jit(solution)/shard_map/ppermute | solution.py:81
  172.2 105.7 %collective-permute-start.1 = (bf16[1,704,2048]{2,1,0:T(8,128)(2,1)}, bf16[1,704,2048]{2,1,0:T(8,128)(2,1)}, u32[]{:S(2)}, u32[]{:S(2)}) collective-permute-start(bf16[1,704,2048]{2,1,0:T(8,128)(2,1)} %param.39), channel_id=1, source_target_pairs={{0,1},{1,0},{2,3},{3,2},{4,5},{5,4},{6,7},{7,6},{8,9},{9,8},{10,11... | collective-permute-start | bytes 8650760 | tf_op jit(solution)/shard_map/ppermute | solution.py:82
  291.2 9.2 %copy-start.4 = (bf16[128,2048]{1,0:T(8,128)(2,1)S(1)}, bf16[128,2048]{1,0:T(8,128)(2,1)}, u32[]{:S(2)}) copy-start(bf16[128,2048]{1,0:T(8,128)(2,1)} %fusion.66) | copy-start | bytes 1572868
  291.2 9.2 %copy-start.10 = (bf16[2048,64]{0,1:T(8,128)(2,1)S(1)}, bf16[2048,64]{0,1:T(8,128)(2,1)}, u32[]{:S(2)}) copy-start(bf16[2048,64]{0,1:T(8,128)(2,1)} %param.34) | copy-start | bytes 786436
  291.2 64.1 %all-to-all-start.2 = ((bf16[64,16,2048]{2,1,0:T(8,128)(2,1)}), bf16[64,16,2048]{2,1,0:T(8,128)(2,1)}, u32[]{:S(2)}, u32[]{:S(2)}) async-start(bf16[64,16,2048]{2,1,0:T(8,128)(2,1)} %bitcast.170), calls=%async_computation.4 | async-start | bytes 8388608 | tf_op jit(solution)/shard_map/all_to_all | solution.py:231
  300.4 59.1 %copy-start.7 = (bf16[128,2048]{1,0:T(8,128)(2,1)S(1)}, bf16[128,2048]{1,0:T(8,128)(2,1)}, u32[]{:S(2)}) copy-start(bf16[128,2048]{1,0:T(8,128)(2,1)} %reduce-scatter.3.cloned.1.call-done) | copy-start | bytes 1572868
  355.3 8.8 %copy-start.1 = (bf16[16,128,512]{2,1,0:T(8,128)(2,1)S(1)}, bf16[16,128,512]{2,1,0:T(8,128)(2,1)}, u32[]{:S(2)}) copy-start(bf16[16,128,512]{2,1,0:T(8,128)(2,1)} %param.29) | copy-start | bytes 6291460
Sparse Core Ops, SparseCore 0:
  9.7 34.0 all-gather.3
  55.4 23.1 all-gather.5
  121.8 30.0 reduce-scatter.2
  155.4 75.9 all-gather.7
  257.3 38.1 reduce-scatter.4
